TPU v7x, 256 devices: a whole 4x4x8 slice. The times are simulated.
256 devices in a mesh: blk: 64 (over z, x, y_hi), aux: 4 (over y_lo, core).
Axes of the slice: x: 4, y: 4 (y_hi: 2, y_lo: 2; y = y_hi * 2 + y_lo), z: 8, core: 2. Of those that a mesh axis runs over, the one named last changes fastest.
Arguments:
- coeffs: bfloat16 [16384, 512], P('blk'), may hold values from -6 to 6
- fitting: bfloat16 [16384, 256, 256], P('blk', 'aux'), may hold values from -0.375 to 0.375
- screen: int32 [256, 4], P('blk'), may hold values from 0 to 255, as said below
- counts: int32 [256], P('blk'), may hold values from 1 to 4, as said below
- tile_order: int32 [64, 16], P('blk'), may hold values from 0 to 15, each once within a row
Outputs:
- fock_tiles: float32 [1024, 4096], P(('blk', 'aux'))
Inputs may be any that keep to these rules, and one draw needn't show every extreme that they name: `screen`: each partner block lies on the same index of blk as its basis block or on one of the two indices before or after it, counted around the axis. `counts`: some block uses all 4 slots and some block only one.
All inputs are finite; a program needn't handle non-finite values.
Results may differ from a plain program's by a relative error of at most 0.0003.
Values may be sent and summed in bfloat16 or wider, within the bound.
A program may use at most 128 MiB of HBM per device.

v0:
```python
import jax
import jax.numpy as jnp
from jax import lax
from jax.sharding import PartitionSpec as P


def passed_along(value, axis, by):
    length = lax.axis_size(axis)
    return lax.ppermute(value, axis, [(i, (i + by) % length) for i in range(length)])


def per_device(coeffs, fitting, screen, counts, tile_order):
    blocks_here = screen.shape[0]
    slot_count = screen.shape[1]
    block_width = coeffs.shape[0] // blocks_here
    orbitals = coeffs.shape[1]
    aux_here = fitting.shape[1]
    loop_size = lax.axis_size("blk")
    position = lax.axis_index("blk")
    earlier = []
    later = []
    moving_up = coeffs
    moving_down = coeffs
    for step in range(2):
        moving_up = passed_along(moving_up, "blk", 1)
        earlier.append(moving_up)
        moving_down = passed_along(moving_down, "blk", -1)
        later.append(moving_down)
    pieces = [earlier[1], earlier[0], coeffs, later[0], later[1]]
    window = jnp.concatenate(pieces, axis=0).reshape(5 * blocks_here, block_width, orbitals)
    owner = screen // blocks_here
    distance = (owner - position + loop_size) % loop_size
    distance = jnp.where(distance > loop_size // 2, distance - loop_size, distance)
    local_block = (distance + 2) * blocks_here + screen % blocks_here
    slot_index = jnp.arange(slot_count, dtype=jnp.int32)
    keep_slot = slot_index[None, :] < counts[:, None]
    picked = jnp.where(
        keep_slot[:, :, None, None], window[local_block], jnp.zeros((), jnp.bfloat16)
    )
    picked = picked.reshape(blocks_here, slot_count * block_width, orbitals)
    fit_blocks = fitting.reshape(blocks_here, block_width, aux_here, slot_count * block_width)
    half = jnp.einsum(
        "mupl,mli->mupi", fit_blocks, picked, preferred_element_type=jnp.float32
    ).astype(jnp.bfloat16)
    flat = half.reshape(blocks_here * block_width, aux_here * orbitals)
    total_aux = aux_here * lax.axis_size("aux")
    gram = lax.dot_general(flat, flat, (((1,), (1,)), ((), ())), preferred_element_type=jnp.float32)
    gram = gram / jnp.sqrt(jnp.float32(total_aux * orbitals))
    tiles = gram.reshape(blocks_here, block_width, blocks_here, block_width).transpose(0, 2, 1, 3)
    tiles = tiles.reshape(blocks_here * blocks_here, block_width * block_width)
    ordered = tiles[tile_order[0]]
    share = ordered.shape[0] // lax.axis_size("aux")
    summed = lax.psum(ordered, "aux")
    return lax.dynamic_slice_in_dim(summed, lax.axis_index("aux") * share, share, 0)


def solution(mesh):
    placed = (P("blk", None), P("blk", "aux", None), P("blk", None), P("blk"), P("blk", None))
    return jax.shard_map(
        per_device, mesh=mesh, in_specs=placed, out_specs=P(("blk", "aux"), None), check_vma=False
    )
```

profile of v0, /device:TPU:1, one launch (start us, length us, event | category | flops | bytes accessed | tf_op | source)
XLA Modules:
  0.0 137.2 jit_solution(14247176783398623179)
XLA Ops:
  6.5 0.0 all-reduce.2.cloned.1.call-start
  6.5 3.7 %collective-permute-start = (bf16[256,512]{1,0:T(8,128)(2,1)}, bf16[256,512]{1,0:T(8,128)(2,1)S(1)}, u32[]{:S(2)}, u32[]{:S(2)}) collective-permute-start(bf16[256,512]{1,0:T(8,128)(2,1)} %param.5), channel_id=1, source_target_pairs={{0,4},{4,8},{8,12},{12,16},{16,20},{20,24},{24,28},{28,32},{32,36}... | collective-permute-start | bytes 786440 | tf_op jit(solution)/shard_map/ppermute | solution.py:9
  10.3 7.5 %collective-permute-start.2 = (bf16[256,512]{1,0:T(8,128)(2,1)}, bf16[256,512]{1,0:T(8,128)(2,1)S(1)}, u32[]{:S(2)}, u32[]{:S(2)}) collective-permute-start(bf16[256,512]{1,0:T(8,128)(2,1)} %param.5), channel_id=1, source_target_pairs={{0,252},{4,0},{8,4},{12,8},{16,12},{20,16},{24,20},{28,24},{32,28}... | collective-permute-start | bytes 786440 | tf_op jit(solution)/shard_map/ppermute | solution.py:9
  17.8 0.7 iota_compare_fusion
  18.5 0.7 compare_select_fusion
  19.2 4.8 %collective-permute-done = bf16[256,512]{1,0:T(8,128)(2,1)S(1)} collective-permute-done((bf16[256,512]{1,0:T(8,128)(2,1)}, bf16[256,512]{1,0:T(8,128)(2,1)S(1)}, u32[]{:S(2)}, u32[]{:S(2)}) %collective-permute-start) | collective-permute-done | bytes 262176 | tf_op jit(solution)/shard_map/ppermute | solution.py:9
  24.0 0.8 collective-permute-start.1
  24.8 0.7 fusion.8
  25.4 0.1 reshape.74
  25.5 0.1 broadcast_in_dim.23
  25.6 0.1 broadcast_in_dim.24
  25.7 0.0 collective-permute-done.2
  25.7 7.6 %collective-permute-start.3 = (bf16[256,512]{1,0:T(8,128)(2,1)S(1)}, bf16[256,512]{1,0:T(8,128)(2,1)S(1)}, u32[]{:S(2)}, u32[]{:S(2)}) collective-permute-start(bf16[256,512]{1,0:T(8,128)(2,1)S(1)} %collective-permute-done.2), channel_id=1, source_target_pairs={{0,252},{4,0},{8,4},{12,8},{16,12},{20,16},{24,20},{28,24},{32,28}... | collective-permute-start | bytes 786440 | tf_op jit(solution)/shard_map/ppermute | solution.py:9
  33.3 4.1 %collective-permute-done.1 = bf16[256,512]{1,0:T(8,128)(2,1)S(1)} collective-permute-done((bf16[256,512]{1,0:T(8,128)(2,1)S(1)}, bf16[256,512]{1,0:T(8,128)(2,1)S(1)}, u32[]{:S(2)}, u32[]{:S(2)}) %collective-permute-start.1) | collective-permute-done | bytes 262176 | tf_op jit(solution)/shard_map/ppermute | solution.py:9
  37.4 1.0 constant_dynamic-update-slice_fusion.2
  38.4 0.0 collective-permute-done.3
  38.4 0.6 gather_fusion
  39.1 0.2 bitcast_select_fusion
  39.3 11.6 %convolution_convert_fusion = bf16[4,512,64,64]{1,3,2,0:T(8,128)(2,1)} fusion(bf16[4,64,64,256]{3,2,1,0:T(8,128)(2,1)} %bitcast.29, bf16[4,256,512]{2,1,0:T(8,128)(2,1)S(1)} %bitcast_select_fusion), kind=kOutput, calls=%fused_computation.2 | convolution fusion | flops 4303355904 | bytes 26214400 | tf_op jit(solution)/shard_map/mupl,mli->mupi/dot_general | solution.py:42
  50.9 18.4 %copy.8 = bf16[32,8,64,512]{3,1,2,0:T(8,128)(2,1)} copy(bf16[32,8,64,512]{3,2,1,0:T(8,128)(2,1)} %bitcast.24) | data formatting | bytes 33554432
  69.3 12.9 %convolution_multiply_fusion = f32[256,256]{1,0:T(8,128)S(1)} fusion(bf16[256,32768]{1,0:T(8,128)(2,1)} %bitcast.25), kind=kOutput, calls=%fused_computation.3 | convolution fusion | flops 4295032832 | bytes 17039360 | tf_op jit(solution)/shard_map/dot_general | solution.py:47
  82.2 0.2 reshape.70
  82.5 0.1 copy.6
  82.6 0.2 reshape.71
  82.7 1.3 gather_fusion.1
  84.1 0.0 all-reduce.2.cloned.1.call-update
  84.1 44.7 %all-reduce.2.cloned.1.call-done = f32[16,4096]{1,0:T(8,128)} async-done(((f32[16,4096]{1,0:T(8,128)}), f32[16,4096]{1,0:T(8,128)}) %all-reduce.2.cloned.1.call-update) | async-done | bytes 262160 | tf_op jit(solution)/shard_map/psum | solution.py:53
  128.8 1.5 %constant_dynamic-slice_fusion = f32[4,4096]{1,0:T(4,128)} fusion(f32[16,4096]{1,0:T(8,128)} %all-reduce.2.cloned.1.call-done, s32[]{:T(128)S(6)} %select_n.47), kind=kLoop, calls=%fused_computation.34 | loop fusion | bytes 131076 | tf_op jit(solution)/shard_map/dynamic_slice | solution.py:54
  (6 shorter events, 0.1 us)
Async XLA Ops:
  6.5 122.2 %all-reduce.2.cloned.1.call-start = ((), (), s32[]{:S(2)}) async-start(), calls=%async_computation | async-start | bytes 524288 | tf_op jit(solution)/shard_map/psum | solution.py:53
  6.5 17.5 %collective-permute-start = (bf16[256,512]{1,0:T(8,128)(2,1)}, bf16[256,512]{1,0:T(8,128)(2,1)S(1)}, u32[]{:S(2)}, u32[]{:S(2)}) collective-permute-start(bf16[256,512]{1,0:T(8,128)(2,1)} %param.5), channel_id=1, source_target_pairs={{0,4},{4,8},{8,12},{12,16},{16,20},{20,24},{24,28},{28,32},{32,36}... | collective-permute-start | bytes 786440 | tf_op jit(solution)/shard_map/ppermute | solution.py:9
  10.3 15.4 %collective-permute-start.2 = (bf16[256,512]{1,0:T(8,128)(2,1)}, bf16[256,512]{1,0:T(8,128)(2,1)S(1)}, u32[]{:S(2)}, u32[]{:S(2)}) collective-permute-start(bf16[256,512]{1,0:T(8,128)(2,1)} %param.5), channel_id=1, source_target_pairs={{0,252},{4,0},{8,4},{12,8},{16,12},{20,16},{24,20},{28,24},{32,28}... | collective-permute-start | bytes 786440 | tf_op jit(solution)/shard_map/ppermute | solution.py:9
  24.0 13.3 %collective-permute-start.1 = (bf16[256,512]{1,0:T(8,128)(2,1)S(1)}, bf16[256,512]{1,0:T(8,128)(2,1)S(1)}, u32[]{:S(2)}, u32[]{:S(2)}) collective-permute-start(bf16[256,512]{1,0:T(8,128)(2,1)S(1)} %collective-permute-done), channel_id=1, source_target_pairs={{0,4},{4,8},{8,12},{12,16},{16,20},{20,24},{24,28},{28,32},{32,36}... | collective-permute-start | bytes 786440 | tf_op jit(solution)/shard_map/ppermute | solution.py:9
  25.7 12.7 %collective-permute-start.3 = (bf16[256,512]{1,0:T(8,128)(2,1)S(1)}, bf16[256,512]{1,0:T(8,128)(2,1)S(1)}, u32[]{:S(2)}, u32[]{:S(2)}) collective-permute-start(bf16[256,512]{1,0:T(8,128)(2,1)S(1)} %collective-permute-done.2), channel_id=1, source_target_pairs={{0,252},{4,0},{8,4},{12,8},{16,12},{20,16},{24,20},{28,24},{32,28}... | collective-permute-start | bytes 786440 | tf_op jit(solution)/shard_map/ppermute | solution.py:9
Sparse Core Ops, SparseCore 0:
  84.2 44.5 all-reduce.1
where the time goes:
time: 138 us; the launch traced here: 137 us
  waiting for transfers between devices  53.6 us (39%)
  matrix products  24.5 us (18%)
  local copies, waits for them, and re-layouts  23.7 us (17%)
  starting transfers between devices  19.6 us (14%)
  between operations  13.5 us (10%)
  other arithmetic  2.3 us (2%)
    psum x1, waiting for transfers between devices, per_device(): summed = lax.psum(ordered, 'aux')  44.7 us
    ppermute x4, starting transfers between devices, passed_along(): lax.ppermute(value, axis, [(i, (i + by) % length) for i in range(length)])  19.6 us
    unnamed x5, local copies, waits for them, and re-layouts  19.5 us
    dot_general x1, matrix products, per_device(): lax.dot_general(flat, flat, (((1,), (1,)), ((), ())), preferred_element_t...  12.9 us
    dot_general x1, matrix products, per_device(): jnp.einsum('mupl,mli->mupi', fit_blocks, picked, preferred_element_type=j...  11.6 us
    ppermute x4, waiting for transfers between devices, passed_along(): lax.ppermute(value, axis, [(i, (i + by) % length) for i in range(length)])  8.87 us
  transfers between devices with their start and end apart: 5, of which 3 were waited for; matrix products, arithmetic and copies ran while one was open for 2% of the time, Pallas kernels for 0%

commit v1 on v0

v1 whole, which is shorter than its diff:
```python
import functools

import jax
import jax.numpy as jnp
from jax import lax
from jax.experimental import pallas as pl
from jax.experimental.pallas import tpu as pltpu
from jax.sharding import PartitionSpec as P

MESH = pl.DeviceIdType.MESH
BF16, F32 = jnp.bfloat16, jnp.float32
CHUNK = 256
STEPS = (-2, -1, 1, 2)


def kernel(
    n_blk, scale, screen, counts, order, coeffs, fitting, out,
    raw, turned, window_a, window_b, picked, half, gram, tiles, ready, first_in, middle, second_in, total,
    load_sem, own_sem, send_sem, near_sem, pass_sem, share_sem, red_send, red_recv,
):
    position = lax.axis_index("blk")
    aux = lax.axis_index("aux")
    y_lo, core = aux // 2, lax.rem(aux, 2)
    blocks, slots = screen.shape
    _, width, orbitals = coeffs.shape
    rows = blocks * width
    aux_here = turned.shape[0]
    chunks = orbitals // CHUNK
    windows = [window_a, window_b]
    share = blocks // 2
    strip = raw.shape[0] // load_sem.shape[0]

    def device(blk, a):
        return {"blk": blk, "aux": a}

    sibling = device(position, y_lo * 2 + 1 - core)
    across = device(position, (1 - y_lo) * 2 + core)
    partners = {}
    for step in STEPS:
        to_aux = aux if step % 2 == 0 else (1 - y_lo) * 2 + core
        partners[step] = device(lax.rem(position + step + n_blk, n_blk), to_aux)

    def load(c):
        at = pl.ds(pl.multiple_of(c * strip, strip), strip)
        return pltpu.make_async_copy(fitting.at[at], raw.at[at], load_sem.at[c])

    for c in range(load_sem.shape[0]):
        load(c).start()
    own = [
        pltpu.make_async_copy(
            coeffs.at[:, :, ch * CHUNK : (ch + 1) * CHUNK],
            windows[ch].at[2 * blocks : 3 * blocks],
            own_sem.at[ch],
        )
        for ch in range(chunks)
    ]
    for copy in own:
        copy.start()

    barrier = pltpu.get_barrier_semaphore()
    everyone = [*partners.values(), sibling, across]
    for who in everyone:
        pl.semaphore_signal(barrier, inc=1, device_id=who, device_id_type=MESH)
    pl.semaphore_wait(barrier, len(everyone))

    sent, passed = {}, {}
    for ch in range(chunks):
        for n, step in enumerate(STEPS):
            lands = windows[ch].at[pl.ds((2 - step) * blocks + core * share, share)]
            sent[ch, n] = pltpu.make_async_remote_copy(
                src_ref=coeffs.at[pl.ds(core * share, share), :, ch * CHUNK : (ch + 1) * CHUNK],
                dst_ref=lands,
                send_sem=send_sem.at[ch, n],
                recv_sem=near_sem.at[ch, n],
                device_id=partners[step],
                device_id_type=MESH,
            )
            sent[ch, n].start()
            passed[ch, n] = pltpu.make_async_remote_copy(
                src_ref=lands,
                dst_ref=lands,
                send_sem=pass_sem.at[ch, n],
                recv_sem=share_sem.at[ch, n],
                device_id=sibling,
                device_id_type=MESH,
            )

    @pl.loop(0, load_sem.shape[0])
    def _(c):
        load(c).wait()
        at = pl.ds(pl.multiple_of(c * strip, strip), strip)
        for p in range(0, aux_here, 16):
            turned[p : p + 16, at, :] = jnp.swapaxes(raw[at, p : p + 16, :], 0, 1)

    def forward(ch):
        for n in range(len(STEPS)):
            sent[ch, n].wait_recv()
            passed[ch, n].start()

    def pick(ch):
        own[ch].wait()
        for n in range(len(STEPS)):
            passed[ch, n].wait_recv()
        for m in range(blocks):
            for s in range(slots):
                block = screen[m, s]
                away = lax.rem(block // blocks - position + 2 + n_blk, n_blk)
                away = jnp.minimum(away, len(STEPS))
                piece = windows[ch][away * blocks + lax.rem(block, blocks)]
                kept = jnp.where(s < counts[m], piece, jnp.zeros_like(piece))
                picked[ch, m, s * width : (s + 1) * width, :] = kept

    def contract(ch):
        for m in range(blocks):
            at = slice(m * width, (m + 1) * width)
            left = turned[:, at, :].reshape(aux_here * width, slots * width)
            got = jnp.dot(left, picked[ch, m], preferred_element_type=F32).astype(BF16)
            half[ch, :, at, :] = got.reshape(aux_here, width, CHUNK)

    def square(ch):
        flat = jnp.concatenate([half[ch, p] for p in range(aux_here)], axis=1)
        got = lax.dot_general(flat, flat, (((1,), (1,)), ((), ())), preferred_element_type=F32)
        for q in range(rows // 128):
            part = got[:, 128 * q : 128 * q + 128]
            gram[q] = part if ch == 0 else gram[q] + part

    forward(0)
    pick(0)
    for ch in range(chunks):
        contract(ch)
        if ch + 1 < chunks:
            forward(ch + 1)
        square(ch)
        if ch + 1 < chunks:
            pick(ch + 1)

    low = lax.broadcasted_iota(jnp.int32, (width // 2, 128), 1) < width
    for j in range(blocks):
        for q in range(rows // 128):
            even = gram[q, pl.ds(j * width, width // 2, stride=2), :]
            odd = gram[q, pl.ds(j * width + 1, width // 2, stride=2), :]
            tiles[j * blocks + 2 * q] = jnp.where(low, even, pltpu.roll(odd, 64, 1))
            tiles[j * blocks + 2 * q + 1] = jnp.where(low, pltpu.roll(even, 64, 1), odd)
    for o in range(tiles.shape[0]):
        ready[(o // 4) % 2, o // 8, o % 4] = tiles[order[0, o]]

    def reduce_copy(src, dst, n, who):
        return pltpu.make_async_remote_copy(
            src_ref=src, dst_ref=dst, send_sem=red_send.at[n], recv_sem=red_recv.at[n],
            device_id=who, device_id_type=MESH,
        )

    far, home = 1 - y_lo, y_lo
    away = reduce_copy(ready.at[1 - core, far], first_in.at[0], 0, sibling)
    here = reduce_copy(ready.at[1 - core, home], first_in.at[1], 1, sibling)
    cross = reduce_copy(middle, second_in, 2, across)
    away.start()
    here.start()
    away.wait_recv()
    middle[...] = ready[core, far] + first_in[0]
    cross.start()
    here.wait_recv()
    total[...] = ready[core, home] + first_in[1]
    cross.wait_recv()
    total[...] = (total[...] + second_in[...]) * scale
    for s in range(total.shape[1]):
        out[:, 128 * s : 128 * s + 128] = total[:, s, :]
    for copy in [*sent.values(), *passed.values(), away, here, cross]:
        copy.wait_send()


def per_device(coeffs, fitting, screen, counts, tile_order):
    rows, orbitals = coeffs.shape
    _, aux_here, inner = fitting.shape
    blocks, _ = screen.shape
    chunks = orbitals // CHUNK
    near = len(STEPS)
    side = rows // blocks
    n_tiles = tile_order.shape[1]
    kept = n_tiles // lax.axis_size("aux")
    tile = (side * side // 128, 128)
    scale = 1.0 / (aux_here * lax.axis_size("aux") * orbitals) ** 0.5
    smem = pl.BlockSpec(memory_space=pltpu.SMEM)
    hbm = pl.BlockSpec(memory_space=pl.ANY)
    return pl.pallas_call(
        functools.partial(kernel, lax.axis_size("blk"), scale),
        out_shape=jax.ShapeDtypeStruct((kept, side * side), F32),
        in_specs=[smem, smem, smem, hbm, hbm],
        out_specs=pl.BlockSpec(memory_space=pltpu.VMEM),
        scratch_shapes=[
            pltpu.VMEM((rows, aux_here, inner), BF16),
            pltpu.VMEM((aux_here, rows, inner), BF16),
            pltpu.VMEM(((near + 1) * blocks, side, CHUNK), BF16),
            pltpu.VMEM(((near + 1) * blocks, side, CHUNK), BF16),
            pltpu.VMEM((chunks, blocks, inner, CHUNK), BF16),
            pltpu.VMEM((chunks, aux_here, rows, CHUNK), BF16),
            pltpu.VMEM((rows // 128, rows, 128), F32),
            pltpu.VMEM((n_tiles, *tile), F32),
            pltpu.VMEM((2, 2, kept, *tile), F32),
            pltpu.VMEM((2, kept, *tile), F32),
            pltpu.VMEM((kept, *tile), F32),
            pltpu.VMEM((kept, *tile), F32),
            pltpu.VMEM((kept, *tile), F32),
            pltpu.SemaphoreType.DMA((16,)),
            pltpu.SemaphoreType.DMA((chunks,)),
            pltpu.SemaphoreType.DMA((chunks, near)),
            pltpu.SemaphoreType.DMA((chunks, near)),
            pltpu.SemaphoreType.DMA((chunks, near)),
            pltpu.SemaphoreType.DMA((chunks, near)),
            pltpu.SemaphoreType.DMA((3,)),
            pltpu.SemaphoreType.DMA((3,)),
        ],
        compiler_params=pltpu.CompilerParams(
            collective_id=0, has_side_effects=True, vmem_limit_bytes=60 << 20
        ),
    )(screen, counts, tile_order, coeffs.reshape(blocks, side, orbitals), fitting)


def solution(mesh):
    placed = (P("blk", None), P("blk", "aux", None), P("blk", None), P("blk"), P("blk", None))
    with jax.sharding.use_abstract_mesh(mesh.abstract_mesh):
        return jax.shard_map(
            per_device, mesh=mesh, in_specs=placed, out_specs=P(("blk", "aux"), None), check_vma=False
        )
```

time: 138 us -> 42.6 us (0.31)
  waiting for transfers between devices: 53.6 us -> 0 us
  Pallas kernels: 0 us -> 41 us
  matrix products: 24.5 us -> 0 us
  local copies, waits for them, and re-layouts: 23.7 us -> 1.47 us
  starting transfers between devices: 19.6 us -> 0 us
  between operations: 13.5 us -> 0.01 us
  other arithmetic: 2.3 us -> 0 us
    psum x1 -> x0, waiting for transfers between devices: 44.7 us -> none  [per_device(): summed = lax.psum(ordered, 'aux')]
    pallas_call x0 -> x1, Pallas kernels: none -> 41 us  [per_device(): pl.pallas_call(functools.partial(kernel, lax.axis_size('blk'), scale), ou...]
    dot_general x2 -> x0, matrix products: 24.5 us -> none  [the longest x1 12.9 us: per_device(): lax.dot_general(flat, flat, (((1,), (1,)), ((), ())), preferred_element_t...]
    ppermute x4 -> x0, starting transfers between devices: 19.6 us -> none  [passed_along(): lax.ppermute(value, axis, [(i, (i + by) % length) for i in range(length)])]
    unnamed x5 -> x1, local copies, waits for them, and re-layouts: 19.5 us -> 1.47 us
    ppermute x4 -> x0, waiting for transfers between devices: 8.87 us -> none  [passed_along(): lax.ppermute(value, axis, [(i, (i + by) % length) for i in range(length)])]
    gather x2 -> x0, local copies, waits for them, and re-layouts: 1.94 us -> none  [the longest x1 1.33 us: per_device(): ordered = tiles[tile_order[0]]]
    select_n x3 -> x0, other arithmetic: 1.57 us -> none  [the longest x1 0.71 us: per_device(): window[local_block]]
  transfers between devices with their start and end apart: 5 -> 0, of which waited for: 3 -> 0; matrix products, arithmetic and copies ran while one was open for 2% -> 0% of each run, Pallas kernels for 0% -> 0%
where the time goes in v1:
time: 42.6 us; the launch traced here: 42.5 us
  Pallas kernels  41 us (96%)
  local copies, waits for them, and re-layouts  1.47 us (3%)
    pallas_call x1, Pallas kernels, per_device(): pl.pallas_call(functools.partial(kernel, lax.axis_size('blk'), scale), ou...  41 us
    unnamed x1, local copies, waits for them, and re-layouts  1.47 us

profile of v1, /device:TPU:1, one launch (start us, length us, event | category | flops | bytes accessed | tf_op | source)
XLA Modules:
  0.0 42.5 jit_solution(9304641944673442654)
XLA Ops:
  0.0 41.0 %shard_map.55 = f32[4,4096]{1,0:T(4,128)} custom-call(s32[4,4]{1,0:T(4,128)} %screen.1, s32[4]{0:T(128)} %counts.1, s32[1,16]{1,0:T(1,128)} %order.1, bf16[4,64,512]{2,1,0:T(8,128)(2,1)} %bitcast.1, bf16[256,64,256]{2,1,0:T(8,128)(2,1)} %fitting.1), custom_call_target="tpu_custom_call" | custom-call | tf_op jit(solution)/shard_map/pallas_call | solution.py:185
  41.0 1.5 %copy.7 = f32[4,4096]{1,0:T(4,128)} copy(f32[4,4096]{1,0:T(4,128)} %shard_map.55) | data formatting | bytes 131072

commit v2 on v1

--- a/solution.py
+++ b/solution.py
@@ -111,19 +111,27 @@
                 picked[ch, m, s * width : (s + 1) * width, :] = kept
 
     def contract(ch):
-        for m in range(blocks):
-            at = slice(m * width, (m + 1) * width)
-            left = turned[:, at, :].reshape(aux_here * width, slots * width)
-            got = jnp.dot(left, picked[ch, m], preferred_element_type=F32).astype(BF16)
-            half[ch, :, at, :] = got.reshape(aux_here, width, CHUNK)
+        @pl.loop(0, blocks // 2)
+        def _(pair):
+            for side in range(2):
+                m = 2 * pair + side
+                at = pl.ds(pl.multiple_of(m * width, width), width)
+                left = turned[:, at, :].reshape(aux_here * width, slots * width)
+                got = jnp.dot(left, picked[ch, m], preferred_element_type=F32).astype(BF16)
+                half[ch, :, at, :] = got.reshape(aux_here, width, CHUNK)
 
     def square(ch):
-        flat = jnp.concatenate([half[ch, p] for p in range(aux_here)], axis=1)
-        got = lax.dot_general(flat, flat, (((1,), (1,)), ((), ())), preferred_element_type=F32)
-        for q in range(rows // 128):
-            part = got[:, 128 * q : 128 * q + 128]
-            gram[q] = part if ch == 0 else gram[q] + part
-
+        depth = aux_here // 2
+
+        @pl.loop(0, 2)
+        def _(part):
+            flat = [half[ch, part * depth + p] for p in range(depth)]
+            flat = jnp.concatenate(flat, axis=1)
+            got = lax.dot_general(flat, flat, (((1,), (1,)), ((), ())), preferred_element_type=F32)
+            for q in range(rows // 128):
+                gram[q] += got[:, 128 * q : 128 * q + 128]
+
+    gram[...] = jnp.zeros_like(gram)
     forward(0)
     pick(0)
     for ch in range(chunks):

time: 42.6 us -> 35.6 us (0.84)
  the two profiles are of different devices: /device:TPU:1 before, /device:TPU:8 now
where the time goes in v2:
time: 35.6 us; the launch traced here: 35.5 us
  Pallas kernels  34 us (96%)
  local copies, waits for them, and re-layouts  1.47 us (4%)
    pallas_call x1, Pallas kernels, per_device(): pl.pallas_call(functools.partial(kernel, lax.axis_size('blk'), scale), ou...  34 us
    unnamed x1, local copies, waits for them, and re-layouts  1.47 us

profile of v2, /device:TPU:8, one launch (start us, length us, event | category | flops | bytes accessed | tf_op | source)
XLA Modules:
  0.0 35.5 jit_solution(16570132961767566666)
XLA Ops:
  0.0 34.0 %shard_map.55 = f32[4,4096]{1,0:T(4,128)} custom-call(s32[4,4]{1,0:T(4,128)} %screen.1, s32[4]{0:T(128)} %counts.1, s32[1,16]{1,0:T(1,128)} %order.1, bf16[4,64,512]{2,1,0:T(8,128)(2,1)} %bitcast.1, bf16[256,64,256]{2,1,0:T(8,128)(2,1)} %fitting.1), custom_call_target="tpu_custom_call" | custom-call | tf_op jit(solution)/shard_map/pallas_call | solution.py:193
  34.0 1.5 %copy.7 = f32[4,4096]{1,0:T(4,128)} copy(f32[4,4096]{1,0:T(4,128)} %shard_map.55) | data formatting | bytes 131072

commit v3 on v2

--- a/solution.py
+++ b/solution.py
@@ -15,7 +15,7 @@
 
 def kernel(
     n_blk, scale, screen, counts, order, coeffs, fitting, out,
-    raw, turned, window_a, window_b, picked, half, gram, tiles, ready, first_in, middle, second_in, total,
+    raw, turned, window_a, window_b, half, gram, tiles, ready, first_in, middle, second_in, total,
     load_sem, own_sem, send_sem, near_sem, pass_sem, share_sem, red_send, red_recv,
 ):
     position = lax.axis_index("blk")
@@ -40,9 +40,48 @@
         to_aux = aux if step % 2 == 0 else (1 - y_lo) * 2 + core
         partners[step] = device(lax.rem(position + step + n_blk, n_blk), to_aux)
 
+    barrier = pltpu.get_barrier_semaphore()
+    everyone = [*partners.values(), sibling, across]
+    for who in everyone:
+        pl.semaphore_signal(barrier, inc=1, device_id=who, device_id_type=MESH)
+
+    places = []
+    for m in range(blocks):
+        places.append([])
+        for s in range(slots):
+            block = screen[m, s]
+            away = lax.rem(block // blocks - position + 2 + n_blk, n_blk)
+            away = jnp.minimum(away, len(STEPS))
+            places[m].append(away * blocks + lax.rem(block, blocks))
+
     def load(c):
         at = pl.ds(pl.multiple_of(c * strip, strip), strip)
         return pltpu.make_async_copy(fitting.at[at], raw.at[at], load_sem.at[c])
+
+    pl.semaphore_wait(barrier, len(everyone))
+
+    sent, passed = {}, {}
+    for ch in range(chunks):
+        for n, step in enumerate(STEPS):
+            lands = windows[ch].at[pl.ds((2 - step) * blocks + core * share, share)]
+            sent[ch, n] = pltpu.make_async_remote_copy(
+                src_ref=coeffs.at[pl.ds(core * share, share), :, ch * CHUNK : (ch + 1) * CHUNK],
+                dst_ref=lands,
+                send_sem=send_sem.at[ch, n],
+                recv_sem=near_sem.at[ch, n],
+                device_id=partners[step],
+                device_id_type=MESH,
+            )
+            if ch == 0:
+                sent[ch, n].start()
+            passed[ch, n] = pltpu.make_async_remote_copy(
+                src_ref=lands,
+                dst_ref=lands,
+                send_sem=pass_sem.at[ch, n],
+                recv_sem=share_sem.at[ch, n],
+                device_id=sibling,
+                device_id_type=MESH,
+            )
 
     for c in range(load_sem.shape[0]):
         load(c).start()
@@ -57,34 +96,6 @@
     for copy in own:
         copy.start()
 
-    barrier = pltpu.get_barrier_semaphore()
-    everyone = [*partners.values(), sibling, across]
-    for who in everyone:
-        pl.semaphore_signal(barrier, inc=1, device_id=who, device_id_type=MESH)
-    pl.semaphore_wait(barrier, len(everyone))
-
-    sent, passed = {}, {}
-    for ch in range(chunks):
-        for n, step in enumerate(STEPS):
-            lands = windows[ch].at[pl.ds((2 - step) * blocks + core * share, share)]
-            sent[ch, n] = pltpu.make_async_remote_copy(
-                src_ref=coeffs.at[pl.ds(core * share, share), :, ch * CHUNK : (ch + 1) * CHUNK],
-                dst_ref=lands,
-                send_sem=send_sem.at[ch, n],
-                recv_sem=near_sem.at[ch, n],
-                device_id=partners[step],
-                device_id_type=MESH,
-            )
-            sent[ch, n].start()
-            passed[ch, n] = pltpu.make_async_remote_copy(
-                src_ref=lands,
-                dst_ref=lands,
-                send_sem=pass_sem.at[ch, n],
-                recv_sem=share_sem.at[ch, n],
-                device_id=sibling,
-                device_id_type=MESH,
-            )
-
     @pl.loop(0, load_sem.shape[0])
     def _(c):
         load(c).wait()
@@ -97,33 +108,33 @@
             sent[ch, n].wait_recv()
             passed[ch, n].start()
 
-    def pick(ch):
+    def arrived(ch):
         own[ch].wait()
         for n in range(len(STEPS)):
             passed[ch, n].wait_recv()
-        for m in range(blocks):
-            for s in range(slots):
-                block = screen[m, s]
-                away = lax.rem(block // blocks - position + 2 + n_blk, n_blk)
-                away = jnp.minimum(away, len(STEPS))
-                piece = windows[ch][away * blocks + lax.rem(block, blocks)]
-                kept = jnp.where(s < counts[m], piece, jnp.zeros_like(piece))
-                picked[ch, m, s * width : (s + 1) * width, :] = kept
+
+    def picked(ch, m):
+        pieces = []
+        for s in range(slots):
+            piece = windows[ch][places[m][s]]
+            pieces.append(jnp.where(s < counts[m], piece, jnp.zeros_like(piece)))
+        return jnp.concatenate(pieces, axis=0)
+
+    once = 1 + position // n_blk
 
     def contract(ch):
-        @pl.loop(0, blocks // 2)
-        def _(pair):
-            for side in range(2):
-                m = 2 * pair + side
-                at = pl.ds(pl.multiple_of(m * width, width), width)
+        @pl.loop(0, once)
+        def _(_):
+            for m in range(blocks):
+                at = slice(m * width, (m + 1) * width)
                 left = turned[:, at, :].reshape(aux_here * width, slots * width)
-                got = jnp.dot(left, picked[ch, m], preferred_element_type=F32).astype(BF16)
+                got = jnp.dot(left, picked(ch, m), preferred_element_type=F32).astype(BF16)
                 half[ch, :, at, :] = got.reshape(aux_here, width, CHUNK)
 
-    def square(ch):
+    def square(ch, parts):
         depth = aux_here // 2
 
-        @pl.loop(0, 2)
+        @pl.loop(parts.start, parts.stop - 1 + once)
         def _(part):
             flat = [half[ch, part * depth + p] for p in range(depth)]
             flat = jnp.concatenate(flat, axis=1)
@@ -132,15 +143,18 @@
                 gram[q] += got[:, 128 * q : 128 * q + 128]
 
     gram[...] = jnp.zeros_like(gram)
+    for n in range(len(STEPS)):
+        sent[0, n].wait_send()
+        sent[1, n].start()
     forward(0)
-    pick(0)
-    for ch in range(chunks):
-        contract(ch)
-        if ch + 1 < chunks:
-            forward(ch + 1)
-        square(ch)
-        if ch + 1 < chunks:
-            pick(ch + 1)
+    arrived(0)
+    contract(0)
+    square(0, range(0, 1))
+    forward(1)
+    square(0, range(1, 2))
+    arrived(1)
+    contract(1)
+    square(1, range(0, 2))
 
     low = lax.broadcasted_iota(jnp.int32, (width // 2, 128), 1) < width
     for j in range(blocks):
@@ -173,7 +187,7 @@
     total[...] = (total[...] + second_in[...]) * scale
     for s in range(total.shape[1]):
         out[:, 128 * s : 128 * s + 128] = total[:, s, :]
-    for copy in [*sent.values(), *passed.values(), away, here, cross]:
+    for copy in [*(sent[1, n] for n in range(len(STEPS))), *passed.values(), away, here, cross]:
         copy.wait_send()
 
 
@@ -192,7 +206,7 @@
     hbm = pl.BlockSpec(memory_space=pl.ANY)
     return pl.pallas_call(
         functools.partial(kernel, lax.axis_size("blk"), scale),
-        out_shape=jax.ShapeDtypeStruct((kept, side * side), F32),
+        out_shape=pltpu.VMEM((kept, side * side), F32),
         in_specs=[smem, smem, smem, hbm, hbm],
         out_specs=pl.BlockSpec(memory_space=pltpu.VMEM),
         scratch_shapes=[
@@ -200,7 +214,6 @@
             pltpu.VMEM((aux_here, rows, inner), BF16),
             pltpu.VMEM(((near + 1) * blocks, side, CHUNK), BF16),
             pltpu.VMEM(((near + 1) * blocks, side, CHUNK), BF16),
-            pltpu.VMEM((chunks, blocks, inner, CHUNK), BF16),
             pltpu.VMEM((chunks, aux_here, rows, CHUNK), BF16),
             pltpu.VMEM((rows // 128, rows, 128), F32),
             pltpu.VMEM((n_tiles, *tile), F32),

time: 35.6 us -> 32.1 us (0.902)
  the two profiles are of different devices: /device:TPU:8 before, /device:TPU:1 now
where the time goes in v3:
time: 32.1 us; the launch traced here: 32 us
  Pallas kernels  31.4 us (98%)
  local copies, waits for them, and re-layouts  0.63 us (2%)
    pallas_call x1, Pallas kernels, per_device(): pl.pallas_call(functools.partial(kernel, lax.axis_size('blk'), scale), ou...  31.4 us

profile of v3, /device:TPU:1, one launch (start us, length us, event | category | flops | bytes accessed | tf_op | source)
XLA Modules:
  0.0 32.0 jit_solution(4863050766197936497)
XLA Ops:
  0.0 31.4 %shard_map.55 = f32[4,4096]{1,0:T(4,128)S(1)} custom-call(s32[4,4]{1,0:T(4,128)} %screen.1, s32[4]{0:T(128)} %counts.1, s32[1,16]{1,0:T(1,128)} %order.1, bf16[4,64,512]{2,1,0:T(8,128)(2,1)} %bitcast.1, bf16[256,64,256]{2,1,0:T(8,128)(2,1)} %fitting.1), custom_call_target="tpu_custom_call" | custom-call | tf_op jit(solution)/shard_map/pallas_call | solution.py:207
  31.4 0.6 %copy.7 = f32[4,4096]{1,0:T(4,128)} copy(f32[4,4096]{1,0:T(4,128)S(1)} %shard_map.55) | data formatting | bytes 131072

commit v4 on v3

--- a/solution.py
+++ b/solution.py
@@ -10,7 +10,7 @@
 MESH = pl.DeviceIdType.MESH
 BF16, F32 = jnp.bfloat16, jnp.float32
 CHUNK = 256
-STEPS = (-2, -1, 1, 2)
+STEPS = (-1, 1, -2, 2)
 
 
 def kernel(
@@ -58,14 +58,26 @@
         at = pl.ds(pl.multiple_of(c * strip, strip), strip)
         return pltpu.make_async_copy(fitting.at[at], raw.at[at], load_sem.at[c])
 
+    own = [
+        pltpu.make_async_copy(
+            coeffs.at[:, :, ch * CHUNK : (ch + 1) * CHUNK],
+            windows[ch].at[2 * blocks : 3 * blocks],
+            own_sem.at[ch],
+        )
+        for ch in range(chunks)
+    ]
+    for copy in own:
+        copy.start()
     pl.semaphore_wait(barrier, len(everyone))
+    for copy in own:
+        copy.wait()
 
     sent, passed = {}, {}
     for ch in range(chunks):
         for n, step in enumerate(STEPS):
             lands = windows[ch].at[pl.ds((2 - step) * blocks + core * share, share)]
             sent[ch, n] = pltpu.make_async_remote_copy(
-                src_ref=coeffs.at[pl.ds(core * share, share), :, ch * CHUNK : (ch + 1) * CHUNK],
+                src_ref=windows[ch].at[pl.ds(2 * blocks + core * share, share)],
                 dst_ref=lands,
                 send_sem=send_sem.at[ch, n],
                 recv_sem=near_sem.at[ch, n],
@@ -85,17 +97,6 @@
 
     for c in range(load_sem.shape[0]):
         load(c).start()
-    own = [
-        pltpu.make_async_copy(
-            coeffs.at[:, :, ch * CHUNK : (ch + 1) * CHUNK],
-            windows[ch].at[2 * blocks : 3 * blocks],
-            own_sem.at[ch],
-        )
-        for ch in range(chunks)
-    ]
-    for copy in own:
-        copy.start()
-
     @pl.loop(0, load_sem.shape[0])
     def _(c):
         load(c).wait()
@@ -104,12 +105,11 @@
             turned[p : p + 16, at, :] = jnp.swapaxes(raw[at, p : p + 16, :], 0, 1)
 
     def forward(ch):
-        for n in range(len(STEPS)):
+        for n in (2, 3, 0, 1):
             sent[ch, n].wait_recv()
             passed[ch, n].start()
 
     def arrived(ch):
-        own[ch].wait()
         for n in range(len(STEPS)):
             passed[ch, n].wait_recv()
 
@@ -131,12 +131,12 @@
                 got = jnp.dot(left, picked(ch, m), preferred_element_type=F32).astype(BF16)
                 half[ch, :, at, :] = got.reshape(aux_here, width, CHUNK)
 
-    def square(ch, parts):
-        depth = aux_here // 2
-
-        @pl.loop(parts.start, parts.stop - 1 + once)
-        def _(part):
-            flat = [half[ch, part * depth + p] for p in range(depth)]
+    def square(ch, part, parts):
+        depth = aux_here // parts
+
+        @pl.loop(part, part + once)
+        def _(at):
+            flat = [half[ch, at * depth + p] for p in range(depth)]
             flat = jnp.concatenate(flat, axis=1)
             got = lax.dot_general(flat, flat, (((1,), (1,)), ((), ())), preferred_element_type=F32)
             for q in range(rows // 128):
@@ -149,12 +149,12 @@
     forward(0)
     arrived(0)
     contract(0)
-    square(0, range(0, 1))
+    square(0, 0, 2)
     forward(1)
-    square(0, range(1, 2))
+    square(0, 1, 2)
     arrived(1)
     contract(1)
-    square(1, range(0, 2))
+    square(1, 0, 1)
 
     low = lax.broadcasted_iota(jnp.int32, (width // 2, 128), 1) < width
     for j in range(blocks):

time: 32.1 us -> 31.6 us (0.984)
  Pallas kernels: 31.4 us -> 30.9 us
    pallas_call x1, Pallas kernels: 31.4 us -> 30.9 us  [per_device(): pl.pallas_call(functools.partial(kernel, lax.axis_size('blk'), scale), ou...]
where the time goes in v4:
time: 31.6 us; the launch traced here: 31.5 us
  Pallas kernels  30.9 us (98%)
  local copies, waits for them, and re-layouts  0.63 us (2%)
    pallas_call x1, Pallas kernels, per_device(): pl.pallas_call(functools.partial(kernel, lax.axis_size('blk'), scale), ou...  30.9 us
    unnamed x1, local copies, waits for them, and re-layouts  0.63 us

profile of v4, /device:TPU:1, one launch (start us, length us, event | category | flops | bytes accessed | tf_op | source)
XLA Modules:
  0.0 31.5 jit_solution(12686484200448286710)
XLA Ops:
  0.0 30.9 %shard_map.55 = f32[4,4096]{1,0:T(4,128)S(1)} custom-call(s32[4,4]{1,0:T(4,128)} %screen.1, s32[4]{0:T(128)} %counts.1, s32[1,16]{1,0:T(1,128)} %order.1, bf16[4,64,512]{2,1,0:T(8,128)(2,1)} %bitcast.1, bf16[256,64,256]{2,1,0:T(8,128)(2,1)} %fitting.1), custom_call_target="tpu_custom_call" | custom-call | tf_op jit(solution)/shard_map/pallas_call | solution.py:207
  30.9 0.6 %copy.7 = f32[4,4096]{1,0:T(4,128)} copy(f32[4,4096]{1,0:T(4,128)S(1)} %shard_map.55) | data formatting | bytes 131072

commit v5 on v4

--- a/solution.py
+++ b/solution.py
@@ -163,8 +163,13 @@
             odd = gram[q, pl.ds(j * width + 1, width // 2, stride=2), :]
             tiles[j * blocks + 2 * q] = jnp.where(low, even, pltpu.roll(odd, 64, 1))
             tiles[j * blocks + 2 * q + 1] = jnp.where(low, pltpu.roll(even, 64, 1), odd)
-    for o in range(tiles.shape[0]):
-        ready[(o // 4) % 2, o // 8, o % 4] = tiles[order[0, o]]
+    far, home = 1 - y_lo, y_lo
+    kept = total.shape[0]
+
+    def lay_out(to_core, to_side):
+        for t in range(kept):
+            o = (to_side * 2 + to_core) * kept + t
+            ready[to_core, to_side, t] = tiles[order[0, o]]
 
     def reduce_copy(src, dst, n, who):
         return pltpu.make_async_remote_copy(
@@ -172,22 +177,31 @@
             device_id=who, device_id_type=MESH,
         )
 
-    far, home = 1 - y_lo, y_lo
     away = reduce_copy(ready.at[1 - core, far], first_in.at[0], 0, sibling)
     here = reduce_copy(ready.at[1 - core, home], first_in.at[1], 1, sibling)
-    cross = reduce_copy(middle, second_in, 2, across)
+    cross = [
+        reduce_copy(middle.at[half_at], second_in.at[half_at], 2 + n, across)
+        for n, half_at in enumerate((pl.ds(0, kept // 2), pl.ds(kept // 2, kept // 2)))
+    ]
+    lay_out(1 - core, far)
     away.start()
+    lay_out(core, far)
+    away.wait_recv()
+    for n in range(2):
+        at = slice(n * (kept // 2), (n + 1) * (kept // 2))
+        middle[at] = ready[core, far, at] + first_in[0, at]
+        cross[n].start()
+    lay_out(1 - core, home)
     here.start()
-    away.wait_recv()
-    middle[...] = ready[core, far] + first_in[0]
-    cross.start()
+    lay_out(core, home)
     here.wait_recv()
     total[...] = ready[core, home] + first_in[1]
-    cross.wait_recv()
+    for copy in cross:
+        copy.wait_recv()
     total[...] = (total[...] + second_in[...]) * scale
     for s in range(total.shape[1]):
         out[:, 128 * s : 128 * s + 128] = total[:, s, :]
-    for copy in [*(sent[1, n] for n in range(len(STEPS))), *passed.values(), away, here, cross]:
+    for copy in [*(sent[1, n] for n in range(len(STEPS))), *passed.values(), away, here, *cross]:
         copy.wait_send()
 
 
@@ -228,8 +242,8 @@
             pltpu.SemaphoreType.DMA((chunks, near)),
             pltpu.SemaphoreType.DMA((chunks, near)),
             pltpu.SemaphoreType.DMA((chunks, near)),
-            pltpu.SemaphoreType.DMA((3,)),
-            pltpu.SemaphoreType.DMA((3,)),
+            pltpu.SemaphoreType.DMA((4,)),
+            pltpu.SemaphoreType.DMA((4,)),
         ],
         compiler_params=pltpu.CompilerParams(
             collective_id=0, has_side_effects=True, vmem_limit_bytes=60 << 20

time: 31.6 us -> 31.6 us (level)
  no operation moved by 1% of the time
where the time goes in v5:
time: 31.6 us; the launch traced here: 31.5 us
  Pallas kernels  30.9 us (98%)
  local copies, waits for them, and re-layouts  0.63 us (2%)
    pallas_call x1, Pallas kernels, per_device(): pl.pallas_call(functools.partial(kernel, lax.axis_size('blk'), scale), ou...  30.9 us
    unnamed x1, local copies, waits for them, and re-layouts  0.63 us

profile of v5, /device:TPU:1, one launch (start us, length us, event | category | flops | bytes accessed | tf_op | source)
XLA Modules:
  0.0 31.5 jit_solution(594376776672985905)
XLA Ops:
  0.0 30.9 %shard_map.55 = f32[4,4096]{1,0:T(4,128)S(1)} custom-call(s32[4,4]{1,0:T(4,128)} %screen.1, s32[4]{0:T(128)} %counts.1, s32[1,16]{1,0:T(1,128)} %order.1, bf16[4,64,512]{2,1,0:T(8,128)(2,1)} %bitcast.1, bf16[256,64,256]{2,1,0:T(8,128)(2,1)} %fitting.1), custom_call_target="tpu_custom_call" | custom-call | tf_op jit(solution)/shard_map/pallas_call | solution.py:221
  30.9 0.6 %copy.7 = f32[4,4096]{1,0:T(4,128)} copy(f32[4,4096]{1,0:T(4,128)S(1)} %shard_map.55) | data formatting | bytes 131072

commit v6 on v5

--- a/solution.py
+++ b/solution.py
@@ -196,12 +196,15 @@
     lay_out(core, home)
     here.wait_recv()
     total[...] = ready[core, home] + first_in[1]
+    for copy in [*(sent[1, n] for n in range(len(STEPS))), *passed.values(), away, here]:
+        copy.wait_send()
+    for n, copy in enumerate(cross):
+        copy.wait_recv()
+        at = slice(n * (kept // 2), (n + 1) * (kept // 2))
+        total[at] = (total[at] + second_in[at]) * scale
+        for s in range(total.shape[1]):
+            out[at, 128 * s : 128 * s + 128] = total[at, s, :]
     for copy in cross:
-        copy.wait_recv()
-    total[...] = (total[...] + second_in[...]) * scale
-    for s in range(total.shape[1]):
-        out[:, 128 * s : 128 * s + 128] = total[:, s, :]
-    for copy in [*(sent[1, n] for n in range(len(STEPS))), *passed.values(), away, here, *cross]:
         copy.wait_send()
 
 

time: 31.6 us -> 31.6 us (level)
  no operation moved by 1% of the time
where the time goes in v6:
time: 31.6 us; the launch traced here: 31.5 us
  Pallas kernels  30.8 us (97%)
  local copies, waits for them, and re-layouts  0.63 us (2%)
    pallas_call x1, Pallas kernels, per_device(): pl.pallas_call(functools.partial(kernel, lax.axis_size('blk'), scale), ou...  30.8 us
    unnamed x1, local copies, waits for them, and re-layouts  0.63 us

profile of v6, /device:TPU:1, one launch (start us, length us, event | category | flops | bytes accessed | tf_op | source)
XLA Modules:
  0.0 31.5 jit_solution(7275648549352696073)
XLA Ops:
  0.0 30.8 %shard_map.55 = f32[4,4096]{1,0:T(4,128)S(1)} custom-call(s32[4,4]{1,0:T(4,128)} %screen.1, s32[4]{0:T(128)} %counts.1, s32[1,16]{1,0:T(1,128)} %order.1, bf16[4,64,512]{2,1,0:T(8,128)(2,1)} %bitcast.1, bf16[256,64,256]{2,1,0:T(8,128)(2,1)} %fitting.1), custom_call_target="tpu_custom_call" | custom-call | tf_op jit(solution)/shard_map/pallas_call | solution.py:224
  30.9 0.6 %copy.7 = f32[4,4096]{1,0:T(4,128)} copy(f32[4,4096]{1,0:T(4,128)S(1)} %shard_map.55) | data formatting | bytes 131072
